TPU v7x, 128 devices: a whole 4x4x4 slice. The times are simulated.
128 devices in a mesh: section: 2 (over x_lo), seq: 8 (over y, core), tp: 8 (over z, x_hi).
Axes of the slice: x: 4 (x_hi: 2, x_lo: 2; x = x_hi * 2 + x_lo), y: 4, z: 4, core: 2. Of those that a mesh axis runs over, the one named last changes fastest.
Arguments:
- hidden_image: bfloat16 [2, 1024, 1536], P(None, 'seq'), may hold values from -6 to 6
- hidden_text: bfloat16 [2, 256, 1536], P(None, 'seq'), may hold values from -6 to 6
- latent: float32 [2, 1024, 64], P(None, 'seq'), may hold values from -6 to 6
- timestep: int32 [2], replicated, may hold values from 14 to 27
- text_length: int32 [2], replicated, may hold values from 64 to 154, as said below
- text_keep: int32 [2, 256], replicated, may hold values 0 or 1
- patch_order: int32 [4], replicated, may hold values from 0 to 3, each once
- stale_image_kv: bfloat16 [2, 2, 1024, 2, 1536], P('section', None, 'seq', None, 'tp'), may hold values from -160 to 160
- stale_text_kv: bfloat16 [2, 2, 256, 2, 1536], P('section', None, 'seq', None, 'tp'), may hold values from -6 to 6
- mod_image: float32 [2, 2, 6, 1536], P('section'), may hold values from -3 to 3
- mod_text: float32 [2, 2, 6, 1536], P('section'), may hold values from -3 to 3
- mod_final: float32 [2, 2, 1536], replicated, may hold values from -3 to 3
- qkv_image: bfloat16 [2, 1536, 3, 1536], P('section', None, None, 'tp'), may hold values from -0.15625 to 0.15625
- out_image: bfloat16 [2, 1536, 1536], P('section', 'tp'), may hold values from -0.15625 to 0.15625
- up_image: bfloat16 [2, 1536, 6144], P('section', None, 'tp'), may hold values from -0.15625 to 0.15625
- down_image: bfloat16 [2, 6144, 1536], P('section', 'tp'), may hold values from -0.078125 to 0.078125
- qkv_text: bfloat16 [2, 1536, 3, 1536], P('section', None, None, 'tp'), may hold values from -0.15625 to 0.15625
- out_text: bfloat16 [2, 1536, 1536], P('section', 'tp'), may hold values from -0.15625 to 0.15625
- up_text: bfloat16 [2, 1536, 6144], P('section', None, 'tp'), may hold values from -0.15625 to 0.15625
- down_text: bfloat16 [2, 6144, 1536], P('section', 'tp'), may hold values from -0.078125 to 0.078125
- final_weight: bfloat16 [1536, 64], replicated, may hold values from -0.3125 to 0.3125
Outputs:
- latent_out: float32 [2, 2, 1024, 64], P('section', None, 'seq')
- image_kv_next: bfloat16 [2, 2, 1024, 2, 1536], P('section', None, 'seq', None, 'tp')
- text_kv_next: bfloat16 [2, 2, 256, 2, 1536], P('section', None, 'seq', None, 'tp')
- text_hidden: bfloat16 [2, 2, 256, 1536], P('section', None, 'seq')
Inputs may be any that keep to these rules, and one draw needn't show every extreme that they name: `text_length`: some request has exactly 154 text tokens.
All inputs are finite; a program needn't handle non-finite values.
Results may differ from a plain program's by a relative error of at most 0.023.
Values may be sent and summed in bfloat16 or wider, within the bound.
No kernel may reach another device: no remote copies, remote signals or barrier semaphores. Data moves between devices by JAX's collectives and lax.ppermute only.
A program may use at most 128 MiB of HBM per device.

v0:
```python
import jax
import jax.numpy as jnp
from jax import lax
from jax.sharding import PartitionSpec as P

HD = 64
STEPS = 28
EPSILON = 1e-06
NEGATIVE = -1e30
TIME_SHIFT = 3.0


def passed_along(value, axis, steps):
    count = lax.axis_size(axis)
    initial, last = (max(0, -steps), min(count, count - steps))
    return lax.ppermute(value, axis, [(source, source + steps) for source in range(initial, last)])


def row_norm(values, shift_rows, scale_rows):
    mean_value = jnp.mean(values, axis=-1, keepdims=True)
    centred = values - mean_value
    variance = jnp.mean(centred * centred, axis=-1, keepdims=True)
    return centred * lax.rsqrt(variance + EPSILON) * (1.0 + scale_rows) + shift_rows


def expand_rows(vectors, row_count):
    return jnp.broadcast_to(
        vectors[:, None, :], (vectors.shape[0], row_count, vectors.shape[1])
    ).reshape(-1, vectors.shape[1])


def project(rows, shift_rows, scale_rows, weight):
    flattened = rows.reshape(-1, rows.shape[-1]).astype(jnp.float32)
    normed = row_norm(flattened, shift_rows, scale_rows).astype(jnp.bfloat16)
    mixed = jnp.dot(
        normed, weight.reshape(weight.shape[0], -1), preferred_element_type=jnp.float32
    ).astype(jnp.bfloat16)
    return mixed.reshape(rows.shape[0], rows.shape[1], 3, -1)


def split_heads(values):
    return values.reshape(values.shape[0], values.shape[1], -1, HD)


def block_scores(queries, keys_block, key_mask):
    scores = jnp.einsum(
        "rqhe,rkhe->rhqk", queries, keys_block, preferred_element_type=jnp.float32
    ) * HD ** (-0.5)
    return jnp.where(key_mask[:, None, None, :], scores, NEGATIVE)


def block_weights(scores, rowmax, values_block, key_mask):
    exponent = jnp.where(key_mask[:, None, None, :], jnp.exp(scores - rowmax[..., None]), 0.0)
    totals = jnp.sum(exponent, axis=-1)
    summed = jnp.einsum(
        "rhqk,rkhe->rhqe",
        exponent.astype(jnp.bfloat16),
        values_block,
        preferred_element_type=jnp.float32,
    )
    return (totals, summed)


def heads_out(totals, summed):
    result = summed / totals[..., None]
    merged = jnp.transpose(result, (0, 2, 1, 3))
    return merged.reshape(result.shape[0], result.shape[2], -1).astype(jnp.bfloat16)


def sigma_of(index_value):
    progress = 1.0 - index_value / STEPS
    return TIME_SHIFT * progress / (1.0 + (TIME_SHIFT - 1.0) * progress)


def on_device(
    hidden_image,
    hidden_text,
    latent,
    timestep,
    text_length,
    text_keep,
    patch_order,
    stale_image_kv,
    stale_text_kv,
    mod_image,
    mod_text,
    mod_final,
    qkv_image,
    out_image,
    up_image,
    down_image,
    qkv_text,
    out_text,
    up_text,
    down_text,
    final_weight,
):
    requests = hidden_image.shape[0]
    model_width = hidden_image.shape[2]
    slot_count = patch_order.shape[0]
    image_local = hidden_image.shape[1]
    text_local = hidden_text.shape[1]
    patch_rows = image_local // slot_count
    group_rows = text_local // slot_count
    slot_rows = patch_rows + group_rows
    local_width = qkv_image.shape[3]
    seq_count = lax.axis_size("seq")
    section_index = lax.axis_index("section")
    first_section = section_index == 0
    text_total = text_keep.shape[1]
    positions = jnp.arange(text_total, dtype=jnp.int32)
    valid_text = (positions[None, :] < text_length[:, None]) & (text_keep == 1)
    stale_image, stale_text = (
        lax.all_gather(stale_image_kv[0], "seq", axis=1, tiled=True),
        lax.all_gather(stale_text_kv[0], "seq", axis=1, tiled=True),
    )
    image_buffer = stale_image.reshape(requests, seq_count, slot_count, patch_rows, 2, local_width)
    text_buffer = stale_text.reshape(requests, seq_count, slot_count, group_rows, 2, local_width)
    image_mrows = [expand_rows(mod_image[0][:, column], patch_rows) for column in range(6)]
    text_mrows = [expand_rows(mod_text[0][:, column], group_rows) for column in range(6)]
    image_input = hidden_image.reshape(requests, slot_count, patch_rows, model_width)
    text_input = hidden_text.reshape(requests, slot_count, group_rows, model_width)
    image_store = jnp.zeros((requests, slot_count, patch_rows, model_width), jnp.bfloat16)
    text_store = jnp.zeros((requests, slot_count, group_rows, model_width), jnp.bfloat16)
    image_kv_store = jnp.zeros((requests, slot_count, patch_rows, 2, local_width), jnp.bfloat16)
    text_kv_store = jnp.zeros((requests, slot_count, group_rows, 2, local_width), jnp.bfloat16)
    arrived_image = jnp.zeros((requests, patch_rows, model_width), jnp.bfloat16)
    arrived_text = jnp.zeros((requests, group_rows, model_width), jnp.bfloat16)
    for moment in range(slot_count + 1):
        slot_raw = moment - section_index
        in_range = (slot_raw >= 0) & (slot_raw < slot_count)
        slot_index = jnp.clip(slot_raw, 0, slot_count - 1)
        patch_index = lax.dynamic_index_in_dim(patch_order, slot_index, 0, keepdims=False)
        image_rows = jnp.where(
            first_section,
            lax.dynamic_index_in_dim(image_input, patch_index, 1, keepdims=False),
            arrived_image,
        )
        text_rows = jnp.where(
            first_section,
            lax.dynamic_index_in_dim(text_input, slot_index, 1, keepdims=False),
            arrived_text,
        )
        image_qkv = project(image_rows, image_mrows[0], image_mrows[1], qkv_image[0])
        text_qkv = project(text_rows, text_mrows[0], text_mrows[1], qkv_text[0])
        fresh_local = jnp.concatenate([image_qkv[:, :, 1:], text_qkv[:, :, 1:]], axis=1)
        queries = split_heads(jnp.concatenate([image_qkv[:, :, 0], text_qkv[:, :, 0]], axis=1))
        fresh_all = lax.all_gather(fresh_local, "seq", axis=1, tiled=True)
        fresh_split = fresh_all.reshape(requests, seq_count, slot_rows, 2, local_width)
        image_buffer = lax.dynamic_update_slice_in_dim(
            image_buffer, fresh_split[:, :, None, :patch_rows], patch_index, axis=2
        )
        text_buffer = lax.dynamic_update_slice_in_dim(
            text_buffer, fresh_split[:, :, None, patch_rows:], slot_index, axis=2
        )
        image_keys = image_buffer.reshape(requests, -1, 2, local_width)
        text_keys = text_buffer.reshape(requests, -1, 2, local_width)
        image_mask = jnp.ones((requests, image_keys.shape[1]), jnp.bool_)
        image_scores = block_scores(queries, split_heads(image_keys[:, :, 0]), image_mask)
        text_scores = block_scores(queries, split_heads(text_keys[:, :, 0]), valid_text)
        rowmax = jnp.maximum(jnp.max(image_scores, axis=-1), jnp.max(text_scores, axis=-1))
        image_totals, image_summed = block_weights(
            image_scores, rowmax, split_heads(image_keys[:, :, 1]), image_mask
        )
        text_totals, text_summed = block_weights(
            text_scores, rowmax, split_heads(text_keys[:, :, 1]), valid_text
        )
        attended = heads_out(image_totals + text_totals, image_summed + text_summed)
        image_part = jnp.dot(
            attended[:, :patch_rows].reshape(-1, local_width),
            out_image[0],
            preferred_element_type=jnp.float32,
        )
        text_part = jnp.dot(
            attended[:, patch_rows:].reshape(-1, local_width),
            out_text[0],
            preferred_element_type=jnp.float32,
        )
        image_flat = image_rows.reshape(-1, model_width).astype(jnp.float32)
        text_flat = text_rows.reshape(-1, model_width).astype(jnp.float32)
        image_sum, text_sum = (
            lax.psum(image_part.astype(jnp.bfloat16), "tp").astype(jnp.float32),
            lax.psum(text_part.astype(jnp.bfloat16), "tp").astype(jnp.float32),
        )
        image_first = image_flat + image_mrows[2] * image_sum
        text_first = text_flat + text_mrows[2] * text_sum
        image_normed = row_norm(image_first, image_mrows[3], image_mrows[4]).astype(jnp.bfloat16)
        text_normed = row_norm(text_first, text_mrows[3], text_mrows[4]).astype(jnp.bfloat16)
        image_hidden = jax.nn.gelu(
            jnp.dot(image_normed, up_image[0], preferred_element_type=jnp.float32), approximate=True
        ).astype(jnp.bfloat16)
        text_hidden_rows = jax.nn.gelu(
            jnp.dot(text_normed, up_text[0], preferred_element_type=jnp.float32), approximate=True
        ).astype(jnp.bfloat16)
        image_down, text_down = (
            lax.psum(
                jnp.dot(image_hidden, down_image[0], preferred_element_type=jnp.float32).astype(
                    jnp.bfloat16
                ),
                "tp",
            ).astype(jnp.float32),
            lax.psum(
                jnp.dot(text_hidden_rows, down_text[0], preferred_element_type=jnp.float32).astype(
                    jnp.bfloat16
                ),
                "tp",
            ).astype(jnp.float32),
        )
        image_new = (image_first + image_mrows[5] * image_down).astype(jnp.bfloat16)
        text_new = (text_first + text_mrows[5] * text_down).astype(jnp.bfloat16)
        image_new_rows = image_new.reshape(requests, patch_rows, model_width)
        text_new_rows = text_new.reshape(requests, group_rows, model_width)
        image_store = jnp.where(
            in_range,
            lax.dynamic_update_index_in_dim(image_store, image_new_rows, patch_index, 1),
            image_store,
        )
        text_store = jnp.where(
            in_range,
            lax.dynamic_update_index_in_dim(text_store, text_new_rows, slot_index, 1),
            text_store,
        )
        image_kv_store = jnp.where(
            in_range,
            lax.dynamic_update_index_in_dim(image_kv_store, image_qkv[:, :, 1:], patch_index, 1),
            image_kv_store,
        )
        text_kv_store = jnp.where(
            in_range,
            lax.dynamic_update_index_in_dim(text_kv_store, text_qkv[:, :, 1:], slot_index, 1),
            text_kv_store,
        )
        if moment < slot_count:
            arrived_image, arrived_text = passed_along(
                (image_new_rows, text_new_rows), "section", 1
            )
    final_rows = image_store.reshape(-1, model_width).astype(jnp.float32)
    final_normed = row_norm(
        final_rows,
        expand_rows(mod_final[:, 0], image_local),
        expand_rows(mod_final[:, 1], image_local),
    ).astype(jnp.bfloat16)
    velocity = jnp.dot(final_normed, final_weight, preferred_element_type=jnp.float32).reshape(
        requests, image_local, -1
    )
    returned = passed_along(velocity.astype(jnp.bfloat16), "section", -1).astype(velocity.dtype)
    velocity_used = jnp.where(first_section, returned, velocity)
    index_value = timestep.astype(jnp.float32)
    sigma_now = sigma_of(index_value)
    sigma_next = sigma_of(index_value + 1.0)
    stepped = latent + (sigma_next - sigma_now)[:, None, None] * velocity_used
    denoised = latent - sigma_now[:, None, None] * velocity_used
    latent_part = jnp.where(first_section, stepped, denoised)[None]
    return (
        latent_part,
        image_kv_store.reshape(requests, image_local, 2, local_width)[None],
        text_kv_store.reshape(requests, text_local, 2, local_width)[None],
        text_store.reshape(requests, text_local, model_width)[None],
    )


def solution(mesh):
    in_specs = (
        P(None, "seq", None),
        P(None, "seq", None),
        P(None, "seq", None),
        P(),
        P(),
        P(),
        P(),
        P("section", None, "seq", None, "tp"),
        P("section", None, "seq", None, "tp"),
        P("section", None, None, None),
        P("section", None, None, None),
        P(),
        P("section", None, None, "tp"),
        P("section", "tp", None),
        P("section", None, "tp"),
        P("section", "tp", None),
        P("section", None, None, "tp"),
        P("section", "tp", None),
        P("section", None, "tp"),
        P("section", "tp", None),
        P(),
    )
    out_specs = (
        P("section", None, "seq", None),
        P("section", None, "seq", None, "tp"),
        P("section", None, "seq", None, "tp"),
        P("section", None, "seq", None),
    )
    return jax.shard_map(
        on_device, mesh=mesh, in_specs=in_specs, out_specs=out_specs, check_vma=False
    )
```

profile of v0, /device:TPU:2, one launch (start us, length us, event | category | flops | bytes accessed | tf_op | source)
XLA Modules:
  0.0 1606.8 jit_solution(7978806751904991760)
XLA Ops:
  25.3 14.3 all-gather.1
  94.2 42.6 %psum.142 = bf16[16,1536]{1,0:T(8,128)(2,1)S(1)} all-reduce(bf16[16,1536]{1,0:T(8,128)(2,1)S(1)} %convolution_convert_fusion.9), channel_id=1, replica_groups=mesh['section'=2,'seq'=8,'tp'=8] {'tp'}, use_global_device_ids=true, to_apply=%region_14.15 | all-reduce | flops 24576 | bytes 98304 | tf_op jit(solution)/shard_map/psum | solution.py:183
  140.6 38.1 %psum.143 = bf16[16,1536]{1,0:T(8,128)(2,1)} all-reduce(bf16[16,1536]{1,0:T(8,128)(2,1)S(1)} %fusion.55), channel_id=1, replica_groups=mesh['section'=2,'seq'=8,'tp'=8] {'tp'}, use_global_device_ids=true, to_apply=%region_17.18 | all-reduce | flops 24576 | bytes 98304 | tf_op jit(solution)/shard_map/psum | solution.py:202
  191.2 77.5 %all-reduce.11.cloned.1.call-done = bf16[64,1536]{1,0:T(8,128)(2,1)} async-done(((bf16[64,1536]{1,0:T(8,128)(2,1)}), bf16[64,1536]{1,0:T(8,128)(2,1)}) %all-reduce.11.cloned.1.call-update) | async-done | bytes 196624 | tf_op jit(solution)/shard_map/psum | solution.py:182
  276.6 81.9 %all-reduce.13.cloned.1.call-done = bf16[64,1536]{1,0:T(8,128)(2,1)} async-done(((bf16[64,1536]{1,0:T(8,128)(2,1)}), bf16[64,1536]{1,0:T(8,128)(2,1)}) %all-reduce.13.cloned.1.call-update) | async-done | bytes 196624 | tf_op jit(solution)/shard_map/psum | solution.py:196
  372.8 13.6 all_gather.24
  414.5 39.5 %psum.146 = bf16[16,1536]{1,0:T(8,128)(2,1)S(1)} all-reduce(bf16[16,1536]{1,0:T(8,128)(2,1)S(1)} %convolution_convert_fusion.8), channel_id=1, replica_groups=mesh['section'=2,'seq'=8,'tp'=8] {'tp'}, use_global_device_ids=true, to_apply=%region_30.31 | all-reduce | flops 24576 | bytes 98304 | tf_op jit(solution)/shard_map/psum | solution.py:183
  458.4 40.0 %psum.147 = bf16[16,1536]{1,0:T(8,128)(2,1)} all-reduce(bf16[16,1536]{1,0:T(8,128)(2,1)} %fusion.58), channel_id=1, replica_groups=mesh['section'=2,'seq'=8,'tp'=8] {'tp'}, use_global_device_ids=true, to_apply=%region_33.34 | all-reduce | flops 24576 | bytes 98304 | tf_op jit(solution)/shard_map/psum | solution.py:202
  510.7 77.7 %all-reduce.15.cloned.1.call-done = bf16[64,1536]{1,0:T(8,128)(2,1)} async-done(((bf16[64,1536]{1,0:T(8,128)(2,1)}), bf16[64,1536]{1,0:T(8,128)(2,1)}) %all-reduce.15.cloned.1.call-update) | async-done | bytes 196624 | tf_op jit(solution)/shard_map/psum | solution.py:182
  597.5 80.7 %all-reduce.17.cloned.1.call-done = bf16[64,1536]{1,0:T(8,128)(2,1)} async-done(((bf16[64,1536]{1,0:T(8,128)(2,1)}), bf16[64,1536]{1,0:T(8,128)(2,1)}) %all-reduce.17.cloned.1.call-update) | async-done | bytes 196624 | tf_op jit(solution)/shard_map/psum | solution.py:196
  692.5 13.8 all_gather.25
  734.4 39.5 %psum.150 = bf16[16,1536]{1,0:T(8,128)(2,1)S(1)} all-reduce(bf16[16,1536]{1,0:T(8,128)(2,1)S(1)} %convolution_convert_fusion.7), channel_id=1, replica_groups=mesh['section'=2,'seq'=8,'tp'=8] {'tp'}, use_global_device_ids=true, to_apply=%region_46.47 | all-reduce | flops 24576 | bytes 98304 | tf_op jit(solution)/shard_map/psum | solution.py:183
  778.3 40.0 %psum.151 = bf16[16,1536]{1,0:T(8,128)(2,1)} all-reduce(bf16[16,1536]{1,0:T(8,128)(2,1)} %fusion.61), channel_id=1, replica_groups=mesh['section'=2,'seq'=8,'tp'=8] {'tp'}, use_global_device_ids=true, to_apply=%region_49.50 | all-reduce | flops 24576 | bytes 98304 | tf_op jit(solution)/shard_map/psum | solution.py:202
  830.6 77.7 %all-reduce.19.cloned.1.call-done = bf16[64,1536]{1,0:T(8,128)(2,1)} async-done(((bf16[64,1536]{1,0:T(8,128)(2,1)}), bf16[64,1536]{1,0:T(8,128)(2,1)}) %all-reduce.19.cloned.1.call-update) | async-done | bytes 196624 | tf_op jit(solution)/shard_map/psum | solution.py:182
  917.3 80.7 %all-reduce.21.cloned.1.call-done = bf16[64,1536]{1,0:T(8,128)(2,1)} async-done(((bf16[64,1536]{1,0:T(8,128)(2,1)}), bf16[64,1536]{1,0:T(8,128)(2,1)}) %all-reduce.21.cloned.1.call-update) | async-done | bytes 196624 | tf_op jit(solution)/shard_map/psum | solution.py:196
  1054.0 39.7 %psum.154 = bf16[16,1536]{1,0:T(8,128)(2,1)S(1)} all-reduce(bf16[16,1536]{1,0:T(8,128)(2,1)S(1)} %convolution_convert_fusion.6), channel_id=1, replica_groups=mesh['section'=2,'seq'=8,'tp'=8] {'tp'}, use_global_device_ids=true, to_apply=%region_62.63 | all-reduce | flops 24576 | bytes 98304 | tf_op jit(solution)/shard_map/psum | solution.py:183
  1098.2 40.0 %psum.155 = bf16[16,1536]{1,0:T(8,128)(2,1)} all-reduce(bf16[16,1536]{1,0:T(8,128)(2,1)} %fusion.64), channel_id=1, replica_groups=mesh['section'=2,'seq'=8,'tp'=8] {'tp'}, use_global_device_ids=true, to_apply=%region_65.66 | all-reduce | flops 24576 | bytes 98304 | tf_op jit(solution)/shard_map/psum | solution.py:202
  1149.1 79.0 %all-reduce.23.cloned.1.call-done = bf16[64,1536]{1,0:T(8,128)(2,1)} async-done(((bf16[64,1536]{1,0:T(8,128)(2,1)}), bf16[64,1536]{1,0:T(8,128)(2,1)}) %all-reduce.23.cloned.1.call-update) | async-done | bytes 196624 | tf_op jit(solution)/shard_map/psum | solution.py:182
  1238.0 79.9 %all-reduce.25.cloned.1.call-done = bf16[64,1536]{1,0:T(8,128)(2,1)} async-done(((bf16[64,1536]{1,0:T(8,128)(2,1)}), bf16[64,1536]{1,0:T(8,128)(2,1)}) %all-reduce.25.cloned.1.call-update) | async-done | bytes 196624 | tf_op jit(solution)/shard_map/psum | solution.py:196
  1332.2 13.6 all_gather.27
  1374.0 39.5 %psum.158 = bf16[16,1536]{1,0:T(8,128)(2,1)S(1)} all-reduce(bf16[16,1536]{1,0:T(8,128)(2,1)S(1)} %convolution_convert_fusion.5), channel_id=1, replica_groups=mesh['section'=2,'seq'=8,'tp'=8] {'tp'}, use_global_device_ids=true, to_apply=%region_78.79 | all-reduce | flops 24576 | bytes 98304 | tf_op jit(solution)/shard_map/psum | solution.py:183
  1419.9 39.8 %psum.159 = bf16[16,1536]{1,0:T(8,128)(2,1)} all-reduce(bf16[16,1536]{1,0:T(8,128)(2,1)} %fusion.67), channel_id=1, replica_groups=mesh['section'=2,'seq'=8,'tp'=8] {'tp'}, use_global_device_ids=true, to_apply=%region_81.82 | all-reduce | flops 24576 | bytes 98304 | tf_op jit(solution)/shard_map/psum | solution.py:202
  1459.7 36.9 %all-reduce.27.cloned.1.call-done = bf16[64,1536]{1,0:T(8,128)(2,1)} async-done(((bf16[64,1536]{1,0:T(8,128)(2,1)}), bf16[64,1536]{1,0:T(8,128)(2,1)}) %all-reduce.27.cloned.1.call-update) | async-done | bytes 196624 | tf_op jit(solution)/shard_map/psum | solution.py:182
  1505.8 80.6 %all-reduce.29.cloned.1.call-done = bf16[64,1536]{1,0:T(8,128)(2,1)} async-done(((bf16[64,1536]{1,0:T(8,128)(2,1)}), bf16[64,1536]{1,0:T(8,128)(2,1)}) %all-reduce.29.cloned.1.call-update) | async-done | bytes 196624 | tf_op jit(solution)/shard_map/psum | solution.py:196
  (591 shorter events, 374.8 us)
Async XLA Ops:
  7.2 265.6 %copy-start = (bf16[1,768,1536]{2,1,0:T(8,128)(2,1)S(1)}, bf16[1,768,1536]{2,1,0:T(8,128)(2,1)}, u32[]{:S(2)}) copy-start(bf16[1,768,1536]{2,1,0:T(8,128)(2,1)} %param.36) | copy-start | bytes 7077892
  7.2 73.1 %all-gather.4.cloned.1.call-start = ((), (), s32[]{:S(2)}) async-start(), calls=%async_computation.10 | async-start | bytes 2359296 | tf_op jit(solution)/shard_map/all_gather | solution.py:114
  9.2 259.5 %all-reduce.11.cloned.1.call-start = ((), (), s32[]{:S(2)}) async-start(), calls=%async_computation | async-start | bytes 393216 | tf_op jit(solution)/shard_map/psum | solution.py:182
  180.3 6.3 collective-permute-start.1
  183.3 175.3 %all-reduce.13.cloned.1.call-start = ((), (), s32[]{:S(2)}) async-start(), calls=%async_computation.1 | async-start | bytes 393216 | tf_op jit(solution)/shard_map/psum | solution.py:196
  276.5 312.0 %all-reduce.15.cloned.1.call-start = ((), (), s32[]{:S(2)}) async-start(), calls=%async_computation.2 | async-start | bytes 393216 | tf_op jit(solution)/shard_map/psum | solution.py:182
  359.7 7.6 collective-permute-start
  458.4 132.2 %copy-start.74 = (f32[2,1536]{1,0:T(2,128)S(1)}, f32[2,1536]{1,0:T(2,128)}, u32[]{:S(2)}) copy-start(f32[2,1536]{1,0:T(2,128)} %get-tuple-element.117) | copy-start | bytes 36868
  458.4 132.3 %copy-start.79 = (f32[2,1536]{1,0:T(2,128)S(1)}, f32[2,1536]{1,0:T(2,128)}, u32[]{:S(2)}) copy-start(f32[2,1536]{1,0:T(2,128)} %get-tuple-element.118) | copy-start | bytes 36868
  499.9 6.2 collective-permute-start.3
  504.9 173.3 %all-reduce.17.cloned.1.call-start = ((), (), s32[]{:S(2)}) async-start(), calls=%async_computation.3 | async-start | bytes 393216 | tf_op jit(solution)/shard_map/psum | solution.py:196
  596.1 312.2 %all-reduce.19.cloned.1.call-start = ((), (), s32[]{:S(2)}) async-start(), calls=%async_computation.4 | async-start | bytes 393216 | tf_op jit(solution)/shard_map/psum | solution.py:182
  679.4 7.6 collective-permute-start.2
  778.3 132.2 %copy-start.80 = (f32[2,1536]{1,0:T(2,128)S(1)}, f32[2,1536]{1,0:T(2,128)}, u32[]{:S(2)}) copy-start(f32[2,1536]{1,0:T(2,128)} %get-tuple-element.118) | copy-start | bytes 36868
  819.8 6.2 collective-permute-start.5
  824.7 173.2 %all-reduce.21.cloned.1.call-start = ((), (), s32[]{:S(2)}) async-start(), calls=%async_computation.5 | async-start | bytes 393216 | tf_op jit(solution)/shard_map/psum | solution.py:196
  915.9 312.2 %all-reduce.23.cloned.1.call-start = ((), (), s32[]{:S(2)}) async-start(), calls=%async_computation.6 | async-start | bytes 393216 | tf_op jit(solution)/shard_map/psum | solution.py:182
  999.2 7.6 collective-permute-start.4
  1139.6 6.2 collective-permute-start.7
  1144.6 173.3 %all-reduce.25.cloned.1.call-start = ((), (), s32[]{:S(2)}) async-start(), calls=%async_computation.7 | async-start | bytes 393216 | tf_op jit(solution)/shard_map/psum | solution.py:196
  1235.8 260.9 %all-reduce.27.cloned.1.call-start = ((), (), s32[]{:S(2)}) async-start(), calls=%async_computation.8 | async-start | bytes 393216 | tf_op jit(solution)/shard_map/psum | solution.py:182
  1319.1 7.6 collective-permute-start.6
  1415.8 170.6 %all-reduce.29.cloned.1.call-start = ((), (), s32[]{:S(2)}) async-start(), calls=%async_computation.9 | async-start | bytes 393216 | tf_op jit(solution)/shard_map/psum | solution.py:196
  1591.9 7.4 collective-permute-start.8
  (101 other events, 4056.7 us)
Sparse Core Ops, SparseCore 0:
  9.7 28.3 all-gather.3
  183.4 85.3 all-reduce.10
  276.6 81.8 all-reduce.12
  505.0 83.3 all-reduce.14
  596.2 81.8 all-reduce.16
  824.9 83.3 all-reduce.18
  916.0 81.8 all-reduce.20
  1144.7 83.3 all-reduce.22
  1235.9 81.8 all-reduce.24
  1415.9 80.6 all-reduce.26
  1504.5 81.8 all-reduce.28
where the time goes:
time: 1620 us; the launch traced here: 1610 us
  waiting for transfers between devices  784 us (48%)
  blocking collectives  481 us (30%)
  local copies, waits for them, and re-layouts  130 us (8%)
  matrix products  100 us (6%)
  other arithmetic  72.3 us (4%)
  between operations  25.4 us (2%)
    psum x5, waiting for transfers between devices, on_device(): lax.psum(jnp.dot(image_hidden, down_image[0], preferred_element_type=jnp....  404 us
    psum x5, waiting for transfers between devices, on_device(): lax.psum(image_part.astype(jnp.bfloat16), 'tp').astype(jnp.float32)  349 us
    psum x5, blocking collectives, on_device(): lax.psum(text_part.astype(jnp.bfloat16), 'tp').astype(jnp.float32)  201 us
    psum x5, blocking collectives, on_device(): lax.psum(jnp.dot(text_hidden_rows, down_text[0], preferred_element_type=j...  198 us
    all_gather x5, blocking collectives, on_device(): fresh_all = lax.all_gather(fresh_local, 'seq', axis=1, tiled=True)  67.8 us
  transfers between devices with their start and end apart: 20, of which 18 were waited for; matrix products, arithmetic and copies ran while one was open for 5% of the time, Pallas kernels for 0%

commit v1 on v0

--- a/solution.py
+++ b/solution.py
@@ -8,6 +8,10 @@
 EPSILON = 1e-06
 NEGATIVE = -1e30
 TIME_SHIFT = 3.0
+
+
+def face_expand(x_in):
+    return jnp.sum(lax.all_gather(x_in, axis_name="tp"), 0)
 
 
 def passed_along(value, axis, steps):
@@ -180,7 +184,7 @@
         text_flat = text_rows.reshape(-1, model_width).astype(jnp.float32)
         image_sum, text_sum = (
             lax.psum(image_part.astype(jnp.bfloat16), "tp").astype(jnp.float32),
-            lax.psum(text_part.astype(jnp.bfloat16), "tp").astype(jnp.float32),
+            face_expand(text_part.astype(jnp.bfloat16)).astype(jnp.float32),
         )
         image_first = image_flat + image_mrows[2] * image_sum
         text_first = text_flat + text_mrows[2] * text_sum

time: 1620 us -> 1570 us (0.969)
  waiting for transfers between devices: 784 us -> 738 us
    psum x5 -> x0, blocking collectives: 201 us -> none  [on_device(): lax.psum(text_part.astype(jnp.bfloat16), 'tp').astype(jnp.float32)]
    all_gather x0 -> x5, blocking collectives: none -> 187 us  [face_expand(): return jnp.sum(lax.all_gather(x_in, axis_name='tp'), 0)]
    psum x5, waiting for transfers between devices: 349 us -> 299 us  [on_device(): lax.psum(image_part.astype(jnp.bfloat16), 'tp').astype(jnp.float32)]
  transfers between devices with their start and end apart: 20 -> 20, of which waited for: 18 -> 17; matrix products, arithmetic and copies ran while one was open for 5% -> 5% of each run, Pallas kernels for 0% -> 0%
where the time goes in v1:
time: 1570 us; the launch traced here: 1560 us
  waiting for transfers between devices  738 us (47%)
  blocking collectives  474 us (30%)
  local copies, waits for them, and re-layouts  127 us (8%)
  matrix products  100 us (6%)
  other arithmetic  77 us (5%)
  between operations  25.5 us (2%)
    psum x5, waiting for transfers between devices, on_device(): lax.psum(jnp.dot(image_hidden, down_image[0], preferred_element_type=jnp....  402 us
    psum x5, waiting for transfers between devices, on_device(): lax.psum(image_part.astype(jnp.bfloat16), 'tp').astype(jnp.float32)  299 us
    psum x5, blocking collectives, on_device(): lax.psum(jnp.dot(text_hidden_rows, down_text[0], preferred_element_type=j...  205 us
    all_gather x5, blocking collectives, face_expand(): return jnp.sum(lax.all_gather(x_in, axis_name='tp'), 0)  187 us
    all_gather x5, blocking collectives, on_device(): fresh_all = lax.all_gather(fresh_local, 'seq', axis=1, tiled=True)  67.8 us
    ppermute x9, waiting for transfers between devices, passed_along(): lax.ppermute(value, axis, [(source, source + steps) for source in range(i...  37 us
  transfers between devices with their start and end apart: 20, of which 17 were waited for; matrix products, arithmetic and copies ran while one was open for 5% of the time, Pallas kernels for 0%

profile of v1, /device:TPU:2, one launch (start us, length us, event | category | flops | bytes accessed | tf_op | source)
XLA Modules:
  0.0 1556.7 jit_solution(11641508024709798911)
XLA Ops:
  24.7 14.3 all-gather.1
  94.3 36.8 %all-gather.2 = bf16[128,1536]{1,0:T(8,128)(2,1)S(1)} all-gather(bf16[16,1536]{1,0:T(8,128)(2,1)S(1)} %convolution_convert_fusion.9), channel_id=4, replica_groups=mesh['section'=2,'seq'=8,'tp'=8] {'tp'}, dimensions={0}, use_global_device_ids=true | all-gather | bytes 442368 | tf_op jit(solution)/shard_map/all_gather | solution.py:14
  135.0 42.2 %psum.107 = bf16[16,1536]{1,0:T(8,128)(2,1)} all-reduce(bf16[16,1536]{1,0:T(8,128)(2,1)S(1)} %fusion.55), channel_id=1, replica_groups=mesh['section'=2,'seq'=8,'tp'=8] {'tp'}, use_global_device_ids=true, to_apply=%region_17.18 | all-reduce | flops 24576 | bytes 98304 | tf_op jit(solution)/shard_map/psum | solution.py:206
  189.7 74.1 %all-reduce.11.cloned.1.call-done = bf16[64,1536]{1,0:T(8,128)(2,1)} async-done(((bf16[64,1536]{1,0:T(8,128)(2,1)}), bf16[64,1536]{1,0:T(8,128)(2,1)}) %all-reduce.11.cloned.1.call-update) | async-done | bytes 196624 | tf_op jit(solution)/shard_map/psum | solution.py:186
  271.6 81.9 %all-reduce.13.cloned.1.call-done = bf16[64,1536]{1,0:T(8,128)(2,1)} async-done(((bf16[64,1536]{1,0:T(8,128)(2,1)}), bf16[64,1536]{1,0:T(8,128)(2,1)}) %all-reduce.13.cloned.1.call-update) | async-done | bytes 196624 | tf_op jit(solution)/shard_map/psum | solution.py:200
  367.8 13.6 all_gather.56
  410.8 37.5 %all-gather.3 = bf16[128,1536]{1,0:T(8,128)(2,1)} all-gather(bf16[16,1536]{1,0:T(8,128)(2,1)S(1)} %convolution_convert_fusion.8), channel_id=5, replica_groups=mesh['section'=2,'seq'=8,'tp'=8] {'tp'}, dimensions={0}, use_global_device_ids=true | all-gather | bytes 442368 | tf_op jit(solution)/shard_map/all_gather | solution.py:14
  453.6 40.9 %psum.110 = bf16[16,1536]{1,0:T(8,128)(2,1)} all-reduce(bf16[16,1536]{1,0:T(8,128)(2,1)} %fusion.58), channel_id=1, replica_groups=mesh['section'=2,'seq'=8,'tp'=8] {'tp'}, use_global_device_ids=true, to_apply=%region_33.34 | all-reduce | flops 24576 | bytes 98304 | tf_op jit(solution)/shard_map/psum | solution.py:206
  506.8 74.8 %all-reduce.15.cloned.1.call-done = bf16[64,1536]{1,0:T(8,128)(2,1)} async-done(((bf16[64,1536]{1,0:T(8,128)(2,1)}), bf16[64,1536]{1,0:T(8,128)(2,1)}) %all-reduce.15.cloned.1.call-update) | async-done | bytes 196624 | tf_op jit(solution)/shard_map/psum | solution.py:186
  590.7 80.7 %all-reduce.17.cloned.1.call-done = bf16[64,1536]{1,0:T(8,128)(2,1)} async-done(((bf16[64,1536]{1,0:T(8,128)(2,1)}), bf16[64,1536]{1,0:T(8,128)(2,1)}) %all-reduce.17.cloned.1.call-update) | async-done | bytes 196624 | tf_op jit(solution)/shard_map/psum | solution.py:200
  685.7 13.8 all_gather.59
  728.8 37.5 %all-gather.4 = bf16[128,1536]{1,0:T(8,128)(2,1)} all-gather(bf16[16,1536]{1,0:T(8,128)(2,1)S(1)} %convolution_convert_fusion.7), channel_id=6, replica_groups=mesh['section'=2,'seq'=8,'tp'=8] {'tp'}, dimensions={0}, use_global_device_ids=true | all-gather | bytes 442368 | tf_op jit(solution)/shard_map/all_gather | solution.py:14
  771.7 40.9 %psum.113 = bf16[16,1536]{1,0:T(8,128)(2,1)} all-reduce(bf16[16,1536]{1,0:T(8,128)(2,1)} %fusion.61), channel_id=1, replica_groups=mesh['section'=2,'seq'=8,'tp'=8] {'tp'}, use_global_device_ids=true, to_apply=%region_49.50 | all-reduce | flops 24576 | bytes 98304 | tf_op jit(solution)/shard_map/psum | solution.py:206
  824.9 74.7 %all-reduce.19.cloned.1.call-done = bf16[64,1536]{1,0:T(8,128)(2,1)} async-done(((bf16[64,1536]{1,0:T(8,128)(2,1)}), bf16[64,1536]{1,0:T(8,128)(2,1)}) %all-reduce.19.cloned.1.call-update) | async-done | bytes 196624 | tf_op jit(solution)/shard_map/psum | solution.py:186
  908.6 80.7 %all-reduce.21.cloned.1.call-done = bf16[64,1536]{1,0:T(8,128)(2,1)} async-done(((bf16[64,1536]{1,0:T(8,128)(2,1)}), bf16[64,1536]{1,0:T(8,128)(2,1)}) %all-reduce.21.cloned.1.call-update) | async-done | bytes 196624 | tf_op jit(solution)/shard_map/psum | solution.py:200
  1003.6 13.6 all_gather.62
  1046.5 37.5 %all-gather.5 = bf16[128,1536]{1,0:T(8,128)(2,1)} all-gather(bf16[16,1536]{1,0:T(8,128)(2,1)S(1)} %convolution_convert_fusion.6), channel_id=7, replica_groups=mesh['section'=2,'seq'=8,'tp'=8] {'tp'}, dimensions={0}, use_global_device_ids=true | all-gather | bytes 442368 | tf_op jit(solution)/shard_map/all_gather | solution.py:14
  1089.4 41.1 %psum.116 = bf16[16,1536]{1,0:T(8,128)(2,1)} all-reduce(bf16[16,1536]{1,0:T(8,128)(2,1)} %fusion.64), channel_id=1, replica_groups=mesh['section'=2,'seq'=8,'tp'=8] {'tp'}, use_global_device_ids=true, to_apply=%region_65.66 | all-reduce | flops 24576 | bytes 98304 | tf_op jit(solution)/shard_map/psum | solution.py:206
  1142.1 75.4 %all-reduce.23.cloned.1.call-done = bf16[64,1536]{1,0:T(8,128)(2,1)} async-done(((bf16[64,1536]{1,0:T(8,128)(2,1)}), bf16[64,1536]{1,0:T(8,128)(2,1)}) %all-reduce.23.cloned.1.call-update) | async-done | bytes 196624 | tf_op jit(solution)/shard_map/psum | solution.py:186
  1227.4 79.9 %all-reduce.25.cloned.1.call-done = bf16[64,1536]{1,0:T(8,128)(2,1)} async-done(((bf16[64,1536]{1,0:T(8,128)(2,1)}), bf16[64,1536]{1,0:T(8,128)(2,1)}) %all-reduce.25.cloned.1.call-update) | async-done | bytes 196624 | tf_op jit(solution)/shard_map/psum | solution.py:200
  1321.6 13.6 all_gather.65
  1364.8 37.7 %all-gather.6 = bf16[128,1536]{1,0:T(8,128)(2,1)} all-gather(bf16[16,1536]{1,0:T(8,128)(2,1)S(1)} %convolution_convert_fusion.5), channel_id=8, replica_groups=mesh['section'=2,'seq'=8,'tp'=8] {'tp'}, dimensions={0}, use_global_device_ids=true | all-gather | bytes 442368 | tf_op jit(solution)/shard_map/all_gather | solution.py:14
  1407.9 40.1 %psum.119 = bf16[16,1536]{1,0:T(8,128)(2,1)S(1)} all-reduce(bf16[16,1536]{1,0:T(8,128)(2,1)} %fusion.67), channel_id=1, replica_groups=mesh['section'=2,'seq'=8,'tp'=8] {'tp'}, use_global_device_ids=true, to_apply=%region_81.82 | all-reduce | flops 24576 | bytes 98304 | tf_op jit(solution)/shard_map/psum | solution.py:206
  1457.2 79.0 %all-reduce.29.cloned.1.call-done = bf16[64,1536]{1,0:T(8,128)(2,1)} async-done(((bf16[64,1536]{1,0:T(8,128)(2,1)}), bf16[64,1536]{1,0:T(8,128)(2,1)}) %all-reduce.29.cloned.1.call-update) | async-done | bytes 196624 | tf_op jit(solution)/shard_map/psum | solution.py:200
  (592 shorter events, 369.0 us)
Async XLA Ops:
  7.2 260.6 %copy-start = (bf16[1,768,1536]{2,1,0:T(8,128)(2,1)S(1)}, bf16[1,768,1536]{2,1,0:T(8,128)(2,1)}, u32[]{:S(2)}) copy-start(bf16[1,768,1536]{2,1,0:T(8,128)(2,1)} %param.36) | copy-start | bytes 7077892
  7.2 73.3 %all-gather.9.cloned.1.call-start = ((), (), s32[]{:S(2)}) async-start(), calls=%async_computation.10 | async-start | bytes 2359296 | tf_op jit(solution)/shard_map/all_gather | solution.py:118
  9.2 254.5 %all-reduce.11.cloned.1.call-start = ((), (), s32[]{:S(2)}) async-start(), calls=%async_computation | async-start | bytes 393216 | tf_op jit(solution)/shard_map/psum | solution.py:186
  22.4 163.7 %copy-start.33 = (f32[2,1536]{1,0:T(2,128)}, f32[2,1536]{1,0:T(2,128)S(1)}, u32[]{:S(2)}) copy-start(f32[2,1536]{1,0:T(2,128)S(1)} %get-tuple-element.115) | copy-start | bytes 36868
  135.0 131.0 %copy-start.62 = (f32[2,1536]{1,0:T(2,128)S(1)}, f32[2,1536]{1,0:T(2,128)}, u32[]{:S(2)}) copy-start(f32[2,1536]{1,0:T(2,128)} %get-tuple-element.117) | copy-start | bytes 36868
  135.0 131.0 %copy-start.67 = (f32[2,1536]{1,0:T(2,128)S(1)}, f32[2,1536]{1,0:T(2,128)}, u32[]{:S(2)}) copy-start(f32[2,1536]{1,0:T(2,128)} %get-tuple-element.118) | copy-start | bytes 36868
  178.7 6.3 collective-permute-start.1
  181.7 171.8 %all-reduce.13.cloned.1.call-start = ((), (), s32[]{:S(2)}) async-start(), calls=%async_computation.1 | async-start | bytes 393216 | tf_op jit(solution)/shard_map/psum | solution.py:200
  271.4 310.2 %all-reduce.15.cloned.1.call-start = ((), (), s32[]{:S(2)}) async-start(), calls=%async_computation.2 | async-start | bytes 393216 | tf_op jit(solution)/shard_map/psum | solution.py:186
  354.7 7.6 collective-permute-start
  496.0 6.2 collective-permute-start.3
  499.0 172.4 %all-reduce.17.cloned.1.call-start = ((), (), s32[]{:S(2)}) async-start(), calls=%async_computation.3 | async-start | bytes 393216 | tf_op jit(solution)/shard_map/psum | solution.py:200
  589.3 310.3 %all-reduce.19.cloned.1.call-start = ((), (), s32[]{:S(2)}) async-start(), calls=%async_computation.4 | async-start | bytes 393216 | tf_op jit(solution)/shard_map/psum | solution.py:186
  672.6 7.6 collective-permute-start.2
  814.1 6.2 collective-permute-start.5
  817.1 172.2 %all-reduce.21.cloned.1.call-start = ((), (), s32[]{:S(2)}) async-start(), calls=%async_computation.5 | async-start | bytes 393216 | tf_op jit(solution)/shard_map/psum | solution.py:200
  907.2 310.3 %all-reduce.23.cloned.1.call-start = ((), (), s32[]{:S(2)}) async-start(), calls=%async_computation.6 | async-start | bytes 393216 | tf_op jit(solution)/shard_map/psum | solution.py:186
  990.5 7.6 collective-permute-start.4
  1132.0 6.2 collective-permute-start.7
  1135.0 172.3 %all-reduce.25.cloned.1.call-start = ((), (), s32[]{:S(2)}) async-start(), calls=%async_computation.7 | async-start | bytes 393216 | tf_op jit(solution)/shard_map/psum | solution.py:200
  1225.2 222.9 %all-reduce.27.cloned.1.call-start = ((), (), s32[]{:S(2)}) async-start(), calls=%async_computation.8 | async-start | bytes 393216 | tf_op jit(solution)/shard_map/psum | solution.py:186
  1308.5 7.6 collective-permute-start.6
  1364.7 171.5 %all-reduce.29.cloned.1.call-start = ((), (), s32[]{:S(2)}) async-start(), calls=%async_computation.9 | async-start | bytes 393216 | tf_op jit(solution)/shard_map/psum | solution.py:200
  1541.7 7.4 collective-permute-start.8
  (99 other events, 4024.0 us)
Sparse Core Ops, SparseCore 0:
  9.7 28.3 all-gather.8
  181.9 81.8 all-reduce.10
  271.6 81.8 all-reduce.12
  499.1 82.4 all-reduce.14
  589.4 81.8 all-reduce.16
  817.2 82.3 all-reduce.18
  907.3 81.8 all-reduce.20
  1135.1 82.3 all-reduce.22
  1225.3 81.8 all-reduce.24
  1364.8 81.2 all-reduce.26
  1455.9 80.3 all-reduce.28
